TPU v7x, 256 devices: a whole 4x4x8 slice. The times are simulated.
256 devices in a mesh: row: 32 (over y, z_lo, core), col: 8 (over x, z_hi).
Axes of the slice: x: 4, y: 4, z: 8 (z_hi: 2, z_lo: 4; z = z_hi * 4 + z_lo), core: 2. Of those that a mesh axis runs over, the one named last changes fastest.
Arguments:
- weight: float32 [8192, 4096], P('row', 'col'), may hold values from -0.0625 to 0.0625
- grad: bfloat16 [8192, 4096], P('row', 'col'), may hold values from -6 to 6
- left: bfloat16 [8192, 8192], P('row', 'col'), may hold values from -0.25 to 3, as said below
- right: bfloat16 [4096, 4096], P('row', 'col'), may hold values from -0.25 to 3, as said below
- tokens: bfloat16 [4096, 8192], P('row'), may hold values from -6 to 6
Outputs:
- new_weight: float32 [8192, 4096], P('row', 'col')
- output: bfloat16 [4096, 4096], P('row', 'col')
Inputs may be any that keep to these rules, and one draw needn't show every extreme that they name: left is symmetric. right is symmetric.
All inputs are finite; a program needn't handle non-finite values.
Results may differ from a plain program's by a relative error of at most 0.0056.
Values may be sent and summed in bfloat16 or wider, within the bound.
A program may use at most 64 MiB of HBM per device.

v0:
```python
import jax
import jax.numpy as jnp
from jax import lax
from jax.sharding import PartitionSpec as P


def shards(weight, grad, left, right, tokens):
    left_panel = lax.all_gather(left, "col", axis=1, tiled=True)
    left_total = jnp.dot(
        left_panel,
        lax.all_gather(grad, "row", axis=0, tiled=True),
        preferred_element_type=jnp.float32,
    )
    left_grad = left_total.astype(jnp.bfloat16)
    right_panel = lax.all_gather(right, "row", axis=0, tiled=True)
    selected = right_panel
    precond = lax.psum_scatter(
        lax.dot_general(
            selected, left_grad, (((1,), (1,)), ((), ())), preferred_element_type=jnp.float32
        ),
        "col",
        scatter_dimension=0,
        tiled=True,
    ).T
    new_weight = weight - 0.01 * precond
    narrow = new_weight.astype(jnp.bfloat16)
    spread = lax.all_to_all(tokens, "row", split_axis=1, concat_axis=0, tiled=True)
    selected = spread
    output = lax.psum_scatter(
        jnp.dot(selected, narrow, preferred_element_type=jnp.float32),
        "row",
        scatter_dimension=0,
        tiled=True,
    )
    return (new_weight, output.astype(jnp.bfloat16))


def solution(mesh):
    return jax.shard_map(
        shards,
        mesh=mesh,
        in_specs=(
            P("row", "col"),
            P("row", "col"),
            P("row", "col"),
            P("row", "col"),
            P("row", None),
        ),
        out_specs=(P("row", "col"), P("row", "col")),
        check_vma=False,
    )
```

profile of v0, /device:TPU:4, one launch (start us, length us, event | category | flops | bytes accessed | tf_op | source)
XLA Modules:
  0.0 573.1 jit_solution(13484413524477637766)
XLA Ops:
  7.2 0.0 all-gather.4.cloned.1.call-start
  7.2 0.7 all-gather.4.cloned.1.call-update
  7.9 0.0 all-gather.8.cloned.1.call-start
  7.9 0.7 all-gather.8.cloned.1.call-update
  8.6 0.0 all-gather.6.cloned.1.call-start
  8.7 0.7 all-gather.6.cloned.1.call-update
  9.4 0.0 reduce-scatter.3.cloned.1.call-start
  9.4 109.7 %all-gather.4.cloned.1.call-done = bf16[256,8192]{1,0:T(8,128)(2,1)} async-done(((bf16[256,1024]{1,0:T(8,128)(2,1)}), bf16[256,8192]{1,0:T(8,128)(2,1)}) %all-gather.4.cloned.1.call-update) | async-done | bytes 4194320 | tf_op jit(solution)/shard_map/all_gather | solution.py:8
  119.1 60.5 %all-gather.8.cloned.1.call-done = bf16[4096,512]{1,0:T(8,128)(2,1)} async-done(((bf16[128,512]{1,0:T(8,128)(2,1)}), bf16[4096,512]{1,0:T(8,128)(2,1)}) %all-gather.8.cloned.1.call-update) | async-done | bytes 4194320 | tf_op jit(solution)/shard_map/all_gather | solution.py:15
  179.6 69.8 %all-gather.6.cloned.1.call-done = bf16[8192,512]{1,0:T(8,128)(2,1)} async-done(((bf16[256,512]{1,0:T(8,128)(2,1)}), bf16[8192,512]{1,0:T(8,128)(2,1)}) %all-gather.6.cloned.1.call-update) | async-done | bytes 8388624 | tf_op jit(solution)/shard_map/all_gather | solution.py:11
  249.4 11.2 %convolution_bitcast_fusion.1 = f32[4096,256]{0,1:T(8,128)} fusion(bf16[4096,512]{1,0:T(8,128)(2,1)} %all-gather.8.cloned.1.call-done, bf16[256,8192]{1,0:T(8,128)(2,1)} %all-gather.4.cloned.1.call-done, bf16[8192,512]{1,0:T(8,128)(2,1)} %all-gather.6.cloned.1.call-done), kind=kOutput, calls=%fused_computation.1 | convolution fusion | flops 3221356544 | bytes 20971520 | tf_op jit(solution)/shard_map/dot_general | solution.py:18
  260.6 0.0 copy-start
  260.6 0.0 reduce-scatter.3.cloned.1.call-update
  260.6 0.0 reduce-scatter.5.cloned.1.call-start
  260.7 1.5 copy-done
  262.2 2.4 copy.9
  264.6 0.0 copy-start.2
  264.6 100.4 %all_to_all.19 = bf16[128,32,256]{0,2,1:T(8,128)(2,1)S(1)} all-to-all(bf16[128,32,256]{0,2,1:T(8,128)(2,1)} %bitcast.14), channel_id=1, replica_groups=mesh['row'=32,'col'=8] {'row'}, dimensions={1} | all-to-all | bytes 4194304 | tf_op jit(solution)/shard_map/all_to_all | solution.py:27
  365.1 2.9 copy.10
  368.0 27.8 %reduce-scatter.3.cloned.1.call-done = f32[512,256]{0,1:T(8,128)} async-done(((f32[4096,256]{0,1:T(8,128)}), f32[512,256]{0,1:T(8,128)}) %reduce-scatter.3.cloned.1.call-update) | async-done | bytes 524304 | tf_op jit(solution)/shard_map/reduce_scatter | solution.py:17
  395.7 0.0 copy-done.2
  395.7 1.1 bitcast_subtract_fusion
  396.9 0.0 copy-start.1
  396.9 6.3 %convolution_bitcast_fusion = f32[4096,512]{0,1:T(8,128)} fusion(bf16[4096,256]{1,0:T(8,128)(2,1)} %bitcast.15, f32[256,512]{1,0:T(8,128)S(1)} %bitcast_subtract_fusion), kind=kOutput, calls=%fused_computation | convolution fusion | flops 1073872896 | bytes 11010048 | tf_op jit(solution)/shard_map/dot_general | solution.py:30
  403.2 0.0 copy-done.1
  403.2 0.0 reduce-scatter.5.cloned.1.call-update
  403.2 161.6 %reduce-scatter.5.cloned.1.call-done = f32[128,512]{0,1:T(8,128)} async-done(((f32[4096,512]{0,1:T(8,128)}), f32[128,512]{0,1:T(8,128)}) %reduce-scatter.5.cloned.1.call-update) | async-done | bytes 262160 | tf_op jit(solution)/shard_map/reduce_scatter | solution.py:29
  564.9 1.0 convert_element_type.11
  565.8 0.8 copy.11
Async XLA Ops:
  7.2 112.0 %all-gather.4.cloned.1.call-start = ((), (), s32[]{:S(2)}) async-start(), calls=%async_computation.3 | async-start | bytes 4718592 | tf_op jit(solution)/shard_map/all_gather | solution.py:8
  7.9 171.7 %all-gather.8.cloned.1.call-start = ((), (), s32[]{:S(2)}) async-start(), calls=%async_computation.5 | async-start | bytes 4325376 | tf_op jit(solution)/shard_map/all_gather | solution.py:15
  8.6 240.7 %all-gather.6.cloned.1.call-start = ((), (), s32[]{:S(2)}) async-start(), calls=%async_computation.4 | async-start | bytes 8650752 | tf_op jit(solution)/shard_map/all_gather | solution.py:11
  9.4 386.4 %reduce-scatter.3.cloned.1.call-start = ((), (), s32[]{:S(2)}) async-start(), calls=%async_computation.6 | async-start | bytes 4718592 | tf_op jit(solution)/shard_map/reduce_scatter | solution.py:17
  260.6 1.6 copy-start
  260.6 304.2 %reduce-scatter.5.cloned.1.call-start = ((), (), s32[]{:S(2)}) async-start(), calls=%async_computation.7 | async-start | bytes 8650752 | tf_op jit(solution)/shard_map/reduce_scatter | solution.py:29
  264.6 131.1 %copy-start.2 = (f32[256,512]{1,0:T(8,128)S(1)}, f32[256,512]{1,0:T(8,128)}, u32[]{:S(2)}) copy-start(f32[256,512]{1,0:T(8,128)} %param.5) | copy-start | bytes 1572868
  396.9 6.3 %copy-start.1 = (f32[256,512]{1,0:T(8,128)}, f32[256,512]{1,0:T(8,128)S(1)}, u32[]{:S(2)}) copy-start(f32[256,512]{1,0:T(8,128)S(1)} %bitcast_subtract_fusion) | copy-start | bytes 1572868
Sparse Core Ops, SparseCore 0:
  10.6 108.4 all-gather.3
  121.0 58.5 all-gather.7
  181.5 67.8 all-gather.5
  260.7 134.9 reduce-scatter.2
  403.3 161.4 reduce-scatter.4
where the time goes:
time: 573 us
  waiting for transfers between devices  431 us (75%)
  blocking collectives  100 us (17%)
  matrix products  17.5 us (3%)
  between operations  13.8 us (2%)
  local copies, waits for them, and re-layouts  7.66 us (1%)
    reduce_scatter x1, waiting for transfers between devices, shards(): lax.psum_scatter(jnp.dot(selected, narrow, preferred_element_type=jnp.flo...  162 us
    all_gather x1, waiting for transfers between devices, shards(): left_panel = lax.all_gather(left, 'col', axis=1, tiled=True)  110 us
    all_to_all x1, blocking collectives, shards(): lax.all_to_all(tokens, 'row', split_axis=1, concat_axis=0, tiled=True)  100 us
    all_gather x1, waiting for transfers between devices, shards(): lax.all_gather(grad, 'row', axis=0, tiled=True)  69.8 us
    all_gather x1, waiting for transfers between devices, shards(): right_panel = lax.all_gather(right, 'row', axis=0, tiled=True)  60.5 us
    reduce_scatter x1, waiting for transfers between devices, shards(): lax.psum_scatter(lax.dot_general(selected, left_grad, (((1,), (1,)), ((),...  27.8 us
  transfers between devices with their start and end apart: 5, of which 5 were waited for; matrix products, arithmetic and copies ran while one was open for 1% of the time, Pallas kernels for 0%

commit v1 on v0

--- a/solution.py
+++ b/solution.py
@@ -24,7 +24,10 @@
     ).T
     new_weight = weight - 0.01 * precond
     narrow = new_weight.astype(jnp.bfloat16)
-    spread = lax.all_to_all(tokens, "row", split_axis=1, concat_axis=0, tiled=True)
+    spread = jnp.concatenate(
+        lax.all_to_all(jnp.stack(jnp.split(tokens, lax.axis_size("row"), axis=1)), "row", 0, 0),
+        axis=0,
+    )
     selected = spread
     output = lax.psum_scatter(
         jnp.dot(selected, narrow, preferred_element_type=jnp.float32),

time: 573 us -> 569 us (level)
  blocking collectives: 100 us -> 0 us
  waiting for transfers between devices: 431 us -> 502 us
  local copies, waits for them, and re-layouts: 7.66 us -> 28.7 us
    all_to_all x1 -> x0, blocking collectives: 100 us -> none  [shards(): lax.all_to_all(tokens, 'row', split_axis=1, concat_axis=0, tiled=True)]
    reduce_scatter x1, waiting for transfers between devices: 27.8 us -> 114 us  [shards(): lax.psum_scatter(lax.dot_general(selected, left_grad, (((1,), (1,)), ((),...]
    unnamed x8 -> x37, local copies, waits for them, and re-layouts: 4.73 us -> 28.1 us
    all_gather x1, waiting for transfers between devices: 110 us -> 94.3 us  [shards(): left_panel = lax.all_gather(left, 'col', axis=1, tiled=True)]
  transfers between devices with their start and end apart: 5 -> 6, of which waited for: 5 -> 5; matrix products, arithmetic and copies ran while one was open for 1% -> 5% of each run, Pallas kernels for 0% -> 0%
where the time goes in v1:
time: 569 us
  waiting for transfers between devices  502 us (88%)
  local copies, waits for them, and re-layouts  28.7 us (5%)
  matrix products  15.7 us (3%)
  between operations  13.8 us (2%)
    reduce_scatter x1, waiting for transfers between devices, shards(): lax.psum_scatter(jnp.dot(selected, narrow, preferred_element_type=jnp.flo...  162 us
    reduce_scatter x1, waiting for transfers between devices, shards(): lax.psum_scatter(lax.dot_general(selected, left_grad, (((1,), (1,)), ((),...  114 us
    all_gather x1, waiting for transfers between devices, shards(): left_panel = lax.all_gather(left, 'col', axis=1, tiled=True)  94.3 us
    all_gather x1, waiting for transfers between devices, shards(): lax.all_gather(grad, 'row', axis=0, tiled=True)  69.8 us
    all_gather x1, waiting for transfers between devices, shards(): right_panel = lax.all_gather(right, 'row', axis=0, tiled=True)  60.5 us
    unnamed x37, local copies, waits for them, and re-layouts  28.1 us
  transfers between devices with their start and end apart: 6, of which 5 were waited for; matrix products, arithmetic and copies ran while one was open for 5% of the time, Pallas kernels for 0%

profile of v1, /device:TPU:4, one launch (start us, length us, event | category | flops | bytes accessed | tf_op | source)
XLA Modules:
  0.0 568.5 jit_solution(5597614680891131559)
XLA Ops:
  7.2 0.0 copy-start.1
  7.2 0.0 all-gather.4.cloned.1.call-start
  7.2 0.7 all-gather.4.cloned.1.call-update
  7.9 0.0 all-gather.8.cloned.1.call-start
  8.0 0.7 all-gather.8.cloned.1.call-update
  8.7 0.0 all-gather.6.cloned.1.call-start
  8.7 0.7 all-gather.6.cloned.1.call-update
  9.4 0.0 reduce-scatter.3.cloned.1.call-start
  9.4 1.5 constant_dynamic-update-slice_fusion.31
  10.9 1.5 constant_dynamic-update-slice_fusion.30
  12.4 1.5 constant_dynamic-update-slice_fusion.29
  13.9 1.5 constant_dynamic-update-slice_fusion.28
  15.3 1.5 constant_dynamic-update-slice_fusion.27
  16.8 1.5 constant_dynamic-update-slice_fusion.26
  18.3 1.5 constant_dynamic-update-slice_fusion.25
  19.7 1.5 constant_dynamic-update-slice_fusion.24
  21.2 1.5 constant_dynamic-update-slice_fusion.23
  22.7 1.5 constant_dynamic-update-slice_fusion.22
  24.2 0.0 copy-done.1
  24.2 0.6 constant_dynamic-update-slice_fusion.21
  24.8 94.3 %all-gather.4.cloned.1.call-done = bf16[256,8192]{1,0:T(8,128)(2,1)} async-done(((bf16[256,1024]{1,0:T(8,128)(2,1)}), bf16[256,8192]{1,0:T(8,128)(2,1)}) %all-gather.4.cloned.1.call-update) | async-done | bytes 4194320 | tf_op jit(solution)/shard_map/all_gather | solution.py:8
  119.1 60.5 %all-gather.8.cloned.1.call-done = bf16[4096,512]{1,0:T(8,128)(2,1)} async-done(((bf16[128,512]{1,0:T(8,128)(2,1)}), bf16[4096,512]{1,0:T(8,128)(2,1)}) %all-gather.8.cloned.1.call-update) | async-done | bytes 4194320 | tf_op jit(solution)/shard_map/all_gather | solution.py:15
  179.6 69.8 %all-gather.6.cloned.1.call-done = bf16[8192,512]{1,0:T(8,128)(2,1)} async-done(((bf16[256,512]{1,0:T(8,128)(2,1)}), bf16[8192,512]{1,0:T(8,128)(2,1)}) %all-gather.6.cloned.1.call-update) | async-done | bytes 8388624 | tf_op jit(solution)/shard_map/all_gather | solution.py:11
  249.4 11.2 %convolution_bitcast_fusion = f32[4096,256]{0,1:T(8,128)} fusion(bf16[4096,512]{1,0:T(8,128)(2,1)} %all-gather.8.cloned.1.call-done, bf16[256,8192]{1,0:T(8,128)(2,1)} %all-gather.4.cloned.1.call-done, bf16[8192,512]{1,0:T(8,128)(2,1)} %all-gather.6.cloned.1.call-done), kind=kOutput, calls=%fused_computation | convolution fusion | flops 3221356544 | bytes 20971520 | tf_op jit(solution)/shard_map/dot_general | solution.py:18
  260.6 0.0 reduce-scatter.3.cloned.1.call-update
  260.6 0.6 constant_dynamic-update-slice_fusion.20
  261.3 0.6 constant_dynamic-update-slice_fusion.19
  261.9 0.6 constant_dynamic-update-slice_fusion.18
  262.5 0.6 constant_dynamic-update-slice_fusion.17
  263.2 0.6 constant_dynamic-update-slice_fusion.16
  263.8 0.6 constant_dynamic-update-slice_fusion.15
  264.4 0.7 constant_dynamic-update-slice_fusion.14
  265.1 0.6 constant_dynamic-update-slice_fusion.13
  265.7 0.6 constant_dynamic-update-slice_fusion.12
  266.4 0.6 constant_dynamic-update-slice_fusion.11
  267.0 0.6 constant_dynamic-update-slice_fusion.10
  267.7 0.6 constant_dynamic-update-slice_fusion.9
  268.3 0.6 constant_dynamic-update-slice_fusion.8
  268.9 0.6 constant_dynamic-update-slice_fusion.7
  269.6 0.6 constant_dynamic-update-slice_fusion.6
  270.2 0.6 constant_dynamic-update-slice_fusion.5
  270.9 0.6 constant_dynamic-update-slice_fusion.4
  271.5 0.6 constant_dynamic-update-slice_fusion.3
  272.1 0.6 constant_dynamic-update-slice_fusion.2
  272.8 0.6 constant_dynamic-update-slice_fusion.1
  273.4 0.6 constant_dynamic-update-slice_fusion
  274.0 0.0 copy-start.2
  274.0 5.2 all-to-all-start
  279.2 0.0 reduce-scatter.5.cloned.1.call-start
  279.3 113.8 %reduce-scatter.3.cloned.1.call-done = f32[512,256]{0,1:T(8,128)} async-done(((f32[4096,256]{0,1:T(8,128)}), f32[512,256]{0,1:T(8,128)}) %reduce-scatter.3.cloned.1.call-update) | async-done | bytes 524304 | tf_op jit(solution)/shard_map/reduce_scatter | solution.py:17
  393.1 0.0 copy-done.2
  393.1 1.1 bitcast_subtract_fusion
  394.2 0.0 copy-start
  394.2 0.0 all-to-all-done
  394.2 4.5 fusion
  398.7 0.0 copy-done
  398.7 0.0 reduce-scatter.5.cloned.1.call-update
  398.7 161.6 %reduce-scatter.5.cloned.1.call-done = f32[128,512]{1,0:T(8,128)} async-done(((f32[4096,512]{1,0:T(8,128)}), f32[128,512]{1,0:T(8,128)}) %reduce-scatter.5.cloned.1.call-update) | async-done | bytes 262160 | tf_op jit(solution)/shard_map/reduce_scatter | solution.py:32
  560.4 1.6 convert_element_type.11
Async XLA Ops:
  7.2 17.0 %copy-start.1 = (bf16[128,8192]{1,0:T(8,128)(2,1)S(1)}, bf16[128,8192]{1,0:T(8,128)(2,1)}, u32[]{:S(2)}) copy-start(bf16[128,8192]{1,0:T(8,128)(2,1)} %param.9) | copy-start | bytes 6291460
  7.2 112.0 %all-gather.4.cloned.1.call-start = ((), (), s32[]{:S(2)}) async-start(), calls=%async_computation.3 | async-start | bytes 4718592 | tf_op jit(solution)/shard_map/all_gather | solution.py:8
  7.9 171.7 %all-gather.8.cloned.1.call-start = ((), (), s32[]{:S(2)}) async-start(), calls=%async_computation.5 | async-start | bytes 4325376 | tf_op jit(solution)/shard_map/all_gather | solution.py:15
  8.7 240.7 %all-gather.6.cloned.1.call-start = ((), (), s32[]{:S(2)}) async-start(), calls=%async_computation.4 | async-start | bytes 8650752 | tf_op jit(solution)/shard_map/all_gather | solution.py:11
  9.4 383.7 %reduce-scatter.3.cloned.1.call-start = ((), (), s32[]{:S(2)}) async-start(), calls=%async_computation.6 | async-start | bytes 4718592 | tf_op jit(solution)/shard_map/reduce_scatter | solution.py:17
  274.0 119.0 %copy-start.2 = (f32[256,512]{1,0:T(8,128)S(1)}, f32[256,512]{1,0:T(8,128)}, u32[]{:S(2)}) copy-start(f32[256,512]{1,0:T(8,128)} %param.5) | copy-start | bytes 1572868
  274.0 120.2 %all-to-all-start = ((bf16[32,128,256]{2,1,0:T(8,128)(2,1)}), bf16[32,128,256]{2,1,0:T(8,128)(2,1)S(1)}, u32[]{:S(2)}, u32[]{:S(2)}) async-start(bf16[32,128,256]{2,1,0:T(8,128)(2,1)} %constant_dynamic-update-slice_fusion), calls=%async_computation.1 | async-start | bytes 4194304 | tf_op jit(solution)/shard_map/all_to_all | solution.py:28
  279.2 281.2 %reduce-scatter.5.cloned.1.call-start = ((), (), s32[]{:S(2)}) async-start(), calls=%async_computation.7 | async-start | bytes 8650752 | tf_op jit(solution)/shard_map/reduce_scatter | solution.py:32
  394.2 4.5 copy-start
Sparse Core Ops, SparseCore 0:
  10.6 108.4 all-gather.3
  121.0 58.5 all-gather.7
  181.5 67.8 all-gather.5
  260.8 132.2 reduce-scatter.2
  398.9 161.4 reduce-scatter.4
